TPU v7x, 32 devices: a whole 2x2x4 slice. The times are simulated.
32 devices in a mesh: field: 2 (over x), tile: 16 (over z, y, core).
Axes of the slice: x: 2, y: 2, z: 4, core: 2. Of those that a mesh axis runs over, the one named last changes fastest.
Arguments:
- psi_det: float32 [128, 8, 8, 128], P(('field', 'tile')), parts along dimension 0, may hold values from -6 to 6
- phi_det: float32 [128, 8, 8, 128], P(('field', 'tile')), parts along dimension 0, may hold values from 0.25 to 4
- dest_tile: int32 [128, 8, 1], P(('field', 'tile')), parts along dimension 0, may hold values from 0 to 15; in each aligned block of 32 rows (0 to 31, 32 to 63, ..., all dimensions but the last counted through in order) at most 4 rows name the same one
- dest_cell: int32 [128, 8], P(('field', 'tile')), parts along dimension 0, may hold values from 0 to 3
- kernel_id: int32 [128, 8], P(('field', 'tile')), parts along dimension 0, may hold values from 0 to 7
- intersection_weight: float32 [128, 8], P(('field', 'tile')), parts along dimension 0, may hold values from 0.5 to 1.5
- kernels: float32 [8, 128, 128], replicated, may hold values from 0 to 2
- row_offsets: int32 [16, 16], P('field'), parts along dimension 0, may hold values from -8 to 8
- col_offsets: int32 [16, 16], P('field'), parts along dimension 0, may hold values from -64 to 64
Outputs:
- best: float32 [256, 512], P(('field', 'tile')), parts along dimension 0
There are 2 independent parts, one for each index of `field`. A program takes and returns all parts, laid end to end along the dimension named above; an argument that names none is the same for every part. Nothing has to cross between parts.
Inputs may be any that keep to these rules, and one draw needn't show every extreme that they name: `dest_tile`: among one device's 4 blocks over all 8 epochs no tile is named more than 4 times, a bound that some block reaches. `kernels`: every kernel is tridiagonal; kernels[k, i, j] = 0 whenever |i - j| > 1.
All inputs are finite; a program needn't handle non-finite values.
Results may differ from a plain program's by a relative error of at most 0.0003.
Values sent between devices are 32-bit elements; how exact they have to be, the bound alone decides.
A program may use at most 64 MiB of HBM per device.

v0:
```python
import functools

import jax
import jax.numpy as jnp
from jax import lax
from jax.experimental import pallas as pl
from jax.experimental.pallas import tpu as pltpu
from jax.sharding import PartitionSpec as P

MESH = pl.DeviceIdType.MESH
LANES = 128
CHUNKS = 2
UNROLL = 4


def split3(x):
    hi = x.astype(jnp.bfloat16)
    rest = x - hi.astype(jnp.float32)
    mid = rest.astype(jnp.bfloat16)
    low = (rest - mid.astype(jnp.float32)).astype(jnp.bfloat16)
    return hi, mid, low


def exact_dot(onehot3, x):
    return jnp.dot(
        onehot3, jnp.concatenate(split3(x), axis=0), preferred_element_type=jnp.float32
    )


def kernel(
    dims,
    psi_ref,
    phi_ref,
    tile_ref,
    cell_ref,
    kid_ref,
    weight_ref,
    kern_ref,
    row_ref,
    col_ref,
    out_ref,
    psi_sums,
    taps,
    moved,
    send,
    recv,
    codes_out,
    codes_in,
    own,
    low,
    high,
    field,
    send_sem,
    recv_sem,
    code_send_sem,
    code_recv_sem,
    self_sem,
    halo_send_sem,
    halo_recv_sem,
):
    n, cap, cells, epochs, rows, kernels, vels = dims
    items = cells * epochs
    slots = n * cap
    pitch = 2 * rows
    part = pitch // CHUNKS
    targets = cells * epochs
    code_lanes = codes_in.shape[2]
    me = lax.axis_index("tile")

    barrier = pltpu.get_barrier_semaphore()

    def greet(step, carry):
        peer = lax.rem(me + step, n)
        pl.semaphore_signal(barrier, inc=1, device_id={"tile": peer}, device_id_type=MESH)
        return carry

    lax.fori_loop(1, n, greet, 0)

    lane = lax.broadcasted_iota(jnp.int32, (8, LANES), 1)
    sub = lax.broadcasted_iota(jnp.int32, (8, LANES), 0)
    for k in range(kernels):
        sums = [jnp.zeros((8, LANES), jnp.float32)] * 3
        for group in range(LANES // 8):
            rows_of = kern_ref[k, pl.ds(group * 8, 8), :]
            gap = lane - sub - group * 8
            sums = [
                jnp.where(gap == off, rows_of, total) for off, total in zip((1, 0, -1), sums)
            ]
        for tap in range(3):
            taps[pl.ds(tap * kernels + k, 1), :] = jnp.sum(sums[tap], axis=0, keepdims=True)

    row_tile = jnp.full((8, LANES), -1, jnp.int32)
    row_code = jnp.zeros((8, LANES), jnp.int32)
    col_tile = [jnp.full((8, LANES), -1, jnp.int32) for _ in range(items // 8)]
    for b in range(cells):
        for e in range(epochs):
            i = b * epochs + e
            kid = kid_ref[b, e]
            weight = weight_ref[b, e]
            before = taps[pl.ds(kid, 1), :] * weight
            centre = taps[pl.ds(kernels + kid, 1), :] * weight
            after = taps[pl.ds(2 * kernels + kid, 1), :] * weight
            for k, ref in enumerate((psi_ref, phi_ref)):
                x = ref[b, e]
                moved[pl.ds(i * pitch + k * rows, rows), :] = (
                    pltpu.roll(x, 1, 1) * before
                    + x * centre
                    + pltpu.roll(x, LANES - 1, 1) * after
                )
            tile = tile_ref[b, e]
            row_tile = jnp.where(lane == i, tile, row_tile)
            row_code = jnp.where(lane == i, cell_ref[b, e] * epochs + e + 1, row_code)
            col_tile[i // 8] = jnp.where(sub == i % 8, tile, col_tile[i // 8])
    col_tile = jnp.concatenate(col_tile, axis=0)
    item_lane = lax.broadcasted_iota(jnp.int32, (items, LANES), 1)
    item_sub = lax.broadcasted_iota(jnp.int32, (items, LANES), 0)
    same = (col_tile == row_tile[0:1, :]).astype(jnp.float32)
    row_rank = jnp.sum(jnp.where(item_sub < item_lane, same, 0.0), axis=0, keepdims=True)
    col_rank = jnp.sum(jnp.where(item_lane < item_sub, same, 0.0), axis=1, keepdims=True)
    row_place = jnp.where(
        row_tile[0:1, :] >= 0, row_tile[0:1, :] * cap + row_rank.astype(jnp.int32), -1
    )
    pick = (
        lax.broadcasted_iota(jnp.int32, (slots, LANES), 0) == row_place
    ).astype(jnp.float32)[:, :items]
    pick3 = jnp.concatenate([pick] * 3, axis=1).astype(jnp.bfloat16)
    for q in range(0, pitch, 2):
        x = jnp.concatenate(
            [moved[pl.ds(q + h, items, stride=pitch), :] for h in range(2)], axis=1
        )
        packed = exact_dot(pick3, x)
        for h in range(2):
            c, r = divmod(q + h, part)
            send[pl.ds(c * slots * part + r, slots, stride=part), :] = packed[:, h * LANES : (h + 1) * LANES]
    named = jnp.where(
        lax.broadcasted_iota(jnp.int32, (n, LANES), 0) == row_tile[0:1, :],
        row_code[0:1, :].astype(jnp.float32),
        0.0,
    )[:, :items].astype(jnp.bfloat16)
    spread = (
        lax.broadcasted_iota(jnp.int32, (items, code_lanes), 1)
        == me * cap + col_rank.astype(jnp.int32)
    ).astype(jnp.bfloat16)
    codes = jnp.dot(named, spread, preferred_element_type=jnp.float32)
    for t in range(n):
        codes_out[t] = codes[t : t + 1, :]

    pl.semaphore_wait(barrier, n - 1)

    span = cap * part

    def block(c, t):
        return pl.ds(pl.multiple_of((c * n + t) * span, span), span)

    def code_copy(peer, slot):
        return pltpu.make_async_remote_copy(
            src_ref=codes_out.at[peer],
            dst_ref=codes_in.at[slot],
            send_sem=code_send_sem.at[peer],
            recv_sem=code_recv_sem.at[slot],
            device_id={"tile": peer},
            device_id_type=MESH,
        )

    def data_copy(c, peer, slot):
        return pltpu.make_async_remote_copy(
            src_ref=send.at[block(c, peer)],
            dst_ref=recv.at[block(c, slot)],
            send_sem=send_sem.at[c, peer],
            recv_sem=recv_sem.at[c, slot],
            device_id={"tile": peer},
            device_id_type=MESH,
        )

    def self_copy(c):
        return pltpu.make_async_copy(
            send.at[block(c, me)], recv.at[block(c, me)], self_sem.at[c]
        )

    def peers(act):
        def step_of(step, carry):
            act(lax.rem(me + step, n))
            return carry

        lax.fori_loop(1, n, step_of, 0, unroll=5)

    def start_chunk(c):
        peers(lambda peer: data_copy(c, peer, me).start())
        self_copy(c).start()

    def finish_chunk(c):
        self_copy(c).wait()
        peers(lambda peer: data_copy(c, peer, peer).wait_recv())

    self_code = pltpu.make_async_copy(codes_out.at[me], codes_in.at[me], self_sem.at[CHUNKS])
    peers(lambda peer: code_copy(peer, me).start())
    self_code.start()
    start_chunk(0)
    start_chunk(1)
    field[...] = jnp.zeros_like(field)

    self_code.wait()
    peers(lambda peer: code_copy(peer, peer).wait_recv())
    code_row = codes_in[0]
    for t in range(1, n):
        code_row = code_row + codes_in[t]
    land = (
        lax.broadcasted_iota(jnp.int32, (targets, code_lanes), 0) + 1
        == code_row.astype(jnp.int32)
    ).astype(jnp.float32)[:, :slots]
    land3 = jnp.concatenate([land] * 3, axis=1).astype(jnp.bfloat16)

    share = targets * part

    def halo(c, way):
        peer = (lax.rem(me + 1, n), lax.rem(me + n - 1, n))[way]
        return pltpu.make_async_remote_copy(
            src_ref=own.at[pl.ds(c * share, share)],
            dst_ref=(low, high)[way].at[pl.ds(c * share, share)],
            send_sem=halo_send_sem.at[way, c],
            recv_sem=halo_recv_sem.at[way, c],
            device_id={"tile": peer},
            device_id_type=MESH,
        )

    def start_halo(c):
        @pl.when(me < n - 1)
        def _():
            halo(c, 0).start()

        @pl.when(me > 0)
        def _():
            halo(c, 1).start()

    def row_at(k, target):
        return ((k * (cells + 2) + 1) * epochs + target) * 3 * rows

    def sum_chunk(c):
        for q in range(0, part, 2):
            x = jnp.concatenate(
                [
                    recv[pl.ds(c * slots * part + q + h, slots, stride=part), :]
                    for h in range(2)
                ],
                axis=1,
            )
            summed = exact_dot(land3, x)
            for h in range(2):
                k, r = divmod(c * part + q + h, rows)
                piece = summed[:, h * LANES : (h + 1) * LANES]
                own[pl.ds(c * share + q + h, targets, stride=part), :] = piece
                field[pl.ds(row_at(k, 0) + rows + r, targets, stride=3 * rows), :] = piece

    def place(ref, c, offset):
        k, r = divmod(c * part, rows)
        for target in range(targets):
            field[pl.ds(row_at(k, target) + offset + r, part), :] = ref[
                pl.ds(c * share + target * part, part), :
            ]

    def finish_halo(c):
        @pl.when(me > 0)
        def _():
            halo(c, 0).wait_recv()
            place(low, c, 0)

        @pl.when(me < n - 1)
        def _():
            halo(c, 1).wait_recv()
            place(high, c, 2 * rows)

    chunk = epochs * 3 * rows

    def stack(k, v):
        sums = [None] * cells
        for e in range(epochs):
            start = LANES + col_ref[e, v]
            skip = start // LANES
            shift = start - skip * LANES
            turn = lax.rem(LANES - shift, LANES)
            base = skip * chunk + e * 3 * rows + rows + row_ref[e, v]
            keep = lane[:rows] < LANES - shift
            turned = [
                pltpu.roll(
                    field[pl.ds(base + (k * (cells + 2) + c) * chunk, rows), :], turn, 1
                )
                for c in range(cells + 1)
            ]
            for c in range(cells):
                piece = jnp.where(keep, turned[c], turned[c + 1])
                sums[c] = piece if e == 0 else sums[c] + piece
        return sums

    def psi_at(v, c):
        return pl.ds(pl.multiple_of((v * cells + c) * rows, rows), rows)

    def psi_stack(v, carry):
        for c, total in enumerate(stack(0, v)):
            psi_sums[psi_at(v, c), :] = total
        return carry

    def phi_stack(v, best):
        sums = stack(1, v)
        return tuple(
            jnp.maximum(
                best[c], psi_sums[psi_at(v, c), :] / jnp.sqrt(jnp.maximum(sums[c], 1.0))
            )
            for c in range(cells)
        )

    half = CHUNKS // 2
    for c in range(CHUNKS):
        finish_chunk(c)
        if c + 2 < CHUNKS:
            start_chunk(c + 2)
        sum_chunk(c)
        start_halo(c)
    for c in range(half):
        finish_halo(c)
    lax.fori_loop(0, vels, psi_stack, 0, unroll=UNROLL)
    for c in range(half, CHUNKS):
        finish_halo(c)

    best = lax.fori_loop(
        0,
        vels,
        phi_stack,
        (jnp.full((rows, LANES), -jnp.inf, jnp.float32),) * cells,
        unroll=UNROLL,
    )
    for c in range(cells):
        out_ref[:, pl.ds(c * LANES, LANES)] = best[c]

    peers(lambda peer: code_copy(peer, me).wait_send())
    for c in range(CHUNKS):
        peers(lambda peer: data_copy(c, peer, me).wait_send())

    @pl.when(me < n - 1)
    def _():
        for c in range(CHUNKS):
            halo(c, 0).wait_send()

    @pl.when(me > 0)
    def _():
        for c in range(CHUNKS):
            halo(c, 1).wait_send()


def body(psi, phi, dest_tile, dest_cell, kernel_id, weight, kernels, row_offsets, col_offsets):
    n = lax.axis_size("tile")
    cells, epochs, rows, width = psi.shape
    items = cells * epochs
    cap = max(2, 2 * items // n)
    slots = n * cap
    vels = row_offsets.shape[1]
    code_lanes = -(-slots // LANES) * LANES
    pitch = 2 * rows
    vmem = pl.BlockSpec(memory_space=pltpu.VMEM)
    smem = pl.BlockSpec(memory_space=pltpu.SMEM)
    f32 = jnp.float32
    return pl.pallas_call(
        functools.partial(
            kernel, (n, cap, cells, epochs, rows, kernels.shape[0], vels)
        ),
        out_shape=pltpu.VMEM((rows, cells * width), f32),
        in_specs=[vmem, vmem, smem, smem, smem, smem, vmem, smem, smem],
        out_specs=vmem,
        scratch_shapes=[
            pltpu.VMEM((vels * cells * rows, width), f32),
            pltpu.VMEM((3 * kernels.shape[0], width), f32),
            pltpu.VMEM((items * pitch, width), f32),
            pltpu.VMEM((slots * pitch, width), f32),
            pltpu.VMEM((slots * pitch, width), f32),
            pltpu.VMEM((n, 1, code_lanes), f32),
            pltpu.VMEM((n, 1, code_lanes), f32),
            pltpu.VMEM((items * pitch, width), f32),
            pltpu.VMEM((items * pitch, width), f32),
            pltpu.VMEM((items * pitch, width), f32),
            pltpu.VMEM((2 * (cells + 2) * epochs * 3 * rows, width), f32),
            pltpu.SemaphoreType.DMA((CHUNKS, n)),
            pltpu.SemaphoreType.DMA((CHUNKS, n)),
            pltpu.SemaphoreType.DMA((n,)),
            pltpu.SemaphoreType.DMA((n,)),
            pltpu.SemaphoreType.DMA((CHUNKS + 1,)),
            pltpu.SemaphoreType.DMA((2, CHUNKS)),
            pltpu.SemaphoreType.DMA((2, CHUNKS)),
        ],
        compiler_params=pltpu.CompilerParams(collective_id=0, has_side_effects=True),
    )(
        psi,
        phi,
        dest_tile.reshape(cells, epochs),
        dest_cell,
        kernel_id,
        weight,
        kernels,
        row_offsets,
        col_offsets,
    )


def solution(mesh):
    placed = (
        P(("field", "tile"), None, None, None),
        P(("field", "tile"), None, None, None),
        P(("field", "tile"), None, None),
        P(("field", "tile"), None),
        P(("field", "tile"), None),
        P(("field", "tile"), None),
        P(),
        P("field", None),
        P("field", None),
    )
    return jax.shard_map(
        body, mesh=mesh, in_specs=placed, out_specs=P(("field", "tile"), None), check_vma=False
    )
```

profile of v0, /device:TPU:1, one launch (start us, length us, event | category | flops | bytes accessed | tf_op | source)
XLA Modules:
  0.0 26.1 jit_solution(3240801775509495841)
XLA Ops:
  0.0 25.5 %shard_map.91 = f32[8,512]{1,0:T(8,128)S(1)} custom-call(f32[4,8,8,128]{3,2,1,0:T(8,128)} %psi_ref.1, f32[4,8,8,128]{3,2,1,0:T(8,128)} %phi_ref.1, s32[4,8]{1,0:T(4,128)} %bitcast.1, s32[4,8]{1,0:T(4,128)} %cell_ref.1, s32[4,8]{1,0:T(4,128)} %kid_ref.1, f32[4,8]{1,0:T(4,128)} %weight_ref.1, f32[8,128,128]{2,1,0:T(8,128)} %kern_ref.1, s32[8,16]{1,0:T(8,128)} %row_ref.1, ...), custom_call_target="tpu_custom_call" | custom-call | tf_op jit(solution)/shard_map/pallas_call | solution.py:361
  25.5 0.6 %copy.11 = f32[8,512]{1,0:T(8,128)} copy(f32[8,512]{1,0:T(8,128)S(1)} %shard_map.91) | data formatting | bytes 32768
where the time goes:
time: 26.3 us; the launch traced here: 26.1 us
  Pallas kernels  25.5 us (97%)
  local copies, waits for them, and re-layouts  0.61 us (2%)
    pallas_call x1, Pallas kernels, body(): pl.pallas_call(functools.partial(kernel, (n, cap, cells, epochs, rows, ke...  25.5 us
    unnamed x1, local copies, waits for them, and re-layouts  0.61 us

commit v1 on v0

v1 whole, which is shorter than its diff:
```python
import functools

import jax
import jax.numpy as jnp
from jax import lax
from jax.experimental import pallas as pl
from jax.experimental.pallas import tpu as pltpu
from jax.sharding import PartitionSpec as P

MESH = pl.DeviceIdType.MESH
LANES = 128
UNROLL = 4


def split2(x):
    hi = x.astype(jnp.bfloat16)
    return hi, (x - hi.astype(jnp.float32)).astype(jnp.bfloat16)


def select_dot(onehot2, x):
    return jnp.dot(
        onehot2, jnp.concatenate(split2(x), axis=0), preferred_element_type=jnp.float32
    )


def kernel(
    dims,
    psi_hbm,
    phi_hbm,
    tile_hbm,
    cell_hbm,
    kid_hbm,
    weight_hbm,
    kern_hbm,
    row_hbm,
    col_hbm,
    out_ref,
    psi_ref,
    phi_ref,
    tile_ref,
    cell_ref,
    kid_ref,
    weight_ref,
    kern_ref,
    row_ref,
    col_ref,
    psi_sums,
    taps,
    moved,
    send,
    recv,
    codes_out,
    codes_in,
    own,
    low,
    high,
    field,
    in_sem,
    send_sem,
    recv_sem,
    code_send_sem,
    code_recv_sem,
    halo_send_sem,
    halo_recv_sem,
    near_sem,
):
    n, cap, cells, epochs, rows, kernels, vels = dims
    items = cells * epochs
    slots = n * cap
    pitch = 2 * rows
    parts = (rows, rows)
    firsts = (0, rows)
    chunks = len(parts)
    targets = cells * epochs
    code_lanes = codes_in.shape[2]
    me = lax.axis_index("tile")
    half = n // 2
    side = me // half

    def across(act):
        def step_of(step, carry):
            act((1 - side) * half + lax.rem(me + step, half))
            return carry

        lax.fori_loop(0, half, step_of, 0, unroll=8)

    def beside(act):
        def step_of(step, carry):
            act(side * half + lax.rem(me + step, half))
            return carry

        lax.fori_loop(1, half, step_of, 0, unroll=7)

    def around(act):
        def step_of(step, carry):
            act(lax.rem(me + step, n))
            return carry

        lax.fori_loop(1, n, step_of, 0, unroll=5)

    barrier = pltpu.get_barrier_semaphore()
    around(
        lambda peer: pl.semaphore_signal(
            barrier, inc=1, device_id={"tile": peer}, device_id_type=MESH
        )
    )

    sources = (tile_hbm, cell_hbm, kid_hbm, weight_hbm, kern_hbm, psi_hbm, phi_hbm, row_hbm, col_hbm)
    places = (tile_ref, cell_ref, kid_ref, weight_ref, kern_ref, psi_ref, phi_ref, row_ref, col_ref)
    loads = [
        pltpu.make_async_copy(source, place, in_sem.at[i])
        for i, (source, place) in enumerate(zip(sources, places))
    ]
    for load in loads:
        load.start()
    field[...] = jnp.zeros_like(field)

    lane = lax.broadcasted_iota(jnp.int32, (8, LANES), 1)
    sub = lax.broadcasted_iota(jnp.int32, (8, LANES), 0)
    loads[4].wait()
    for k in range(kernels):
        sums = [jnp.zeros((8, LANES), jnp.float32)] * 3
        for group in range(LANES // 8):
            rows_of = kern_ref[k, pl.ds(group * 8, 8), :]
            gap = lane - sub - group * 8
            sums = [
                jnp.where(gap == off, rows_of, total) for off, total in zip((1, 0, -1), sums)
            ]
        for tap in range(3):
            taps[pl.ds(tap * kernels + k, 1), :] = jnp.sum(sums[tap], axis=0, keepdims=True)

    for load in loads[:4]:
        load.wait()
    row_tile = jnp.full((8, LANES), -1, jnp.int32)
    row_code = jnp.zeros((8, LANES), jnp.int32)
    col_tile = [jnp.full((8, LANES), -1, jnp.int32) for _ in range(items // 8)]
    for b in range(cells):
        for e in range(epochs):
            i = b * epochs + e
            tile = tile_ref[b, e]
            row_tile = jnp.where(lane == i, tile, row_tile)
            row_code = jnp.where(lane == i, cell_ref[b, e] * epochs + e + 1, row_code)
            col_tile[i // 8] = jnp.where(sub == i % 8, tile, col_tile[i // 8])

    def move(k, ref):
        for b in range(cells):
            for e in range(epochs):
                i = b * epochs + e
                kid = kid_ref[b, e]
                weight = weight_ref[b, e]
                before = taps[pl.ds(kid, 1), :] * weight
                centre = taps[pl.ds(kernels + kid, 1), :] * weight
                after = taps[pl.ds(2 * kernels + kid, 1), :] * weight
                x = ref[b, e]
                moved[pl.ds(i * pitch + k * rows, rows), :] = (
                    pltpu.roll(x, 1, 1) * before
                    + x * centre
                    + pltpu.roll(x, LANES - 1, 1) * after
                )

    col_tile = jnp.concatenate(col_tile, axis=0)
    item_lane = lax.broadcasted_iota(jnp.int32, (items, LANES), 1)
    item_sub = lax.broadcasted_iota(jnp.int32, (items, LANES), 0)
    same = (col_tile == row_tile[0:1, :]).astype(jnp.float32)
    row_rank = jnp.sum(jnp.where(item_sub < item_lane, same, 0.0), axis=0, keepdims=True)
    col_rank = jnp.sum(jnp.where(item_lane < item_sub, same, 0.0), axis=1, keepdims=True)
    row_place = jnp.where(
        row_tile[0:1, :] >= 0, row_tile[0:1, :] * cap + row_rank.astype(jnp.int32), -1
    )
    pick = (
        lax.broadcasted_iota(jnp.int32, (slots, LANES), 0) == row_place
    ).astype(jnp.float32)[:, :items]
    pick2 = jnp.concatenate([pick] * 2, axis=1).astype(jnp.bfloat16)

    def block(c, t):
        span = cap * parts[c]
        return pl.ds(pl.multiple_of(slots * firsts[c] + t * span, span), span)

    def pack(c):
        for q in range(0, parts[c], 2):
            x = jnp.concatenate(
                [
                    moved[pl.ds(firsts[c] + q + h, items, stride=pitch), :]
                    for h in range(2)
                ],
                axis=1,
            )
            packed = select_dot(pick2, x)
            for h in range(2):
                send[pl.ds(slots * firsts[c] + q + h, slots, stride=parts[c]), :] = packed[
                    :, h * LANES : (h + 1) * LANES
                ]
        recv[block(c, me), :] = send[block(c, me), :]

    loads[5].wait()
    move(0, psi_ref)
    pack(0)
    named = jnp.where(
        lax.broadcasted_iota(jnp.int32, (n, LANES), 0) == row_tile[0:1, :],
        row_code[0:1, :].astype(jnp.float32),
        0.0,
    )[:, :items].astype(jnp.bfloat16)
    spread = (
        lax.broadcasted_iota(jnp.int32, (items, code_lanes), 1)
        == me * cap + col_rank.astype(jnp.int32)
    ).astype(jnp.bfloat16)
    codes = jnp.dot(named, spread, preferred_element_type=jnp.float32)
    for t in range(n):
        codes_out[t] = codes[t : t + 1, :]

    codes_in[me] = codes_out[me]

    def code_copy(peer):
        return pltpu.make_async_remote_copy(
            src_ref=codes_out.at[peer],
            dst_ref=codes_in.at[me],
            send_sem=code_send_sem,
            recv_sem=code_recv_sem,
            device_id={"tile": peer},
            device_id_type=MESH,
        )

    def all_codes():
        return pltpu.make_async_remote_copy(
            src_ref=codes_out.at[pl.ds(0, n - 1)],
            dst_ref=codes_in.at[pl.ds(0, n - 1)],
            send_sem=code_send_sem,
            recv_sem=code_recv_sem,
            device_id={"tile": lax.rem(me + 1, n)},
            device_id_type=MESH,
        )

    def data_copy(c, peer):
        return pltpu.make_async_remote_copy(
            src_ref=send.at[block(c, peer)],
            dst_ref=recv.at[block(c, me)],
            send_sem=send_sem.at[c],
            recv_sem=recv_sem.at[c],
            device_id={"tile": peer},
            device_id_type=MESH,
        )

    def all_data(c):
        rest = pl.ds(slots * firsts[c], (n - 1) * cap * parts[c])
        return pltpu.make_async_remote_copy(
            src_ref=send.at[rest],
            dst_ref=recv.at[rest],
            send_sem=send_sem.at[c],
            recv_sem=recv_sem.at[c],
            device_id={"tile": lax.rem(me + 1, n)},
            device_id_type=MESH,
        )

    def start_codes(peer):
        code_copy(peer).start()

    def start_data(c):
        return lambda peer: data_copy(c, peer).start()

    pl.semaphore_wait(barrier, n - 1)
    around(start_codes)
    around(start_data(0))
    loads[6].wait()
    move(1, phi_ref)
    for c in range(1, chunks):
        pack(c)
        around(start_data(c))
    for load in loads[7:]:
        load.wait()

    all_codes().wait_recv()
    code_row = codes_in[0]
    for t in range(1, n):
        code_row = code_row + codes_in[t]
    land = (
        lax.broadcasted_iota(jnp.int32, (targets, code_lanes), 0) + 1
        == code_row.astype(jnp.int32)
    ).astype(jnp.float32)[:, :slots]
    land2 = jnp.concatenate([land] * 2, axis=1).astype(jnp.bfloat16)

    def share(c):
        return pl.ds(targets * firsts[c], targets * parts[c])

    def halo(c, way):
        peer = (lax.rem(me + 1, n), lax.rem(me + n - 1, n))[way]
        return pltpu.make_async_remote_copy(
            src_ref=own.at[share(c)],
            dst_ref=(low, high)[way].at[share(c)],
            send_sem=halo_send_sem.at[way, c],
            recv_sem=halo_recv_sem.at[way, c],
            device_id={"tile": peer},
            device_id_type=MESH,
        )

    def start_halo(c):
        @pl.when(me < n - 1)
        def _():
            halo(c, 0).start()

        @pl.when(me > 0)
        def _():
            halo(c, 1).start()

    def row_at(k, target):
        return ((k * (cells + 2) + 1) * epochs + target) * 3 * rows

    def sum_chunk(c):
        part = parts[c]
        for q in range(0, part, 2):
            x = jnp.concatenate(
                [
                    recv[pl.ds(slots * firsts[c] + q + h, slots, stride=part), :]
                    for h in range(2)
                ],
                axis=1,
            )
            summed = select_dot(land2, x)
            for h in range(2):
                k, r = divmod(firsts[c] + q + h, rows)
                piece = summed[:, h * LANES : (h + 1) * LANES]
                own[pl.ds(targets * firsts[c] + q + h, targets, stride=part), :] = piece
                field[pl.ds(row_at(k, 0) + rows + r, targets, stride=3 * rows), :] = piece

    def place(ref, c, offset):
        part = parts[c]
        k, r = divmod(firsts[c], rows)
        for target in range(targets):
            field[pl.ds(row_at(k, target) + offset + r, part), :] = ref[
                pl.ds(targets * firsts[c] + target * part, part), :
            ]

    def finish_halo(c):
        @pl.when(me > 0)
        def _():
            halo(c, 0).wait_recv()
            place(low, c, 0)

        @pl.when(me < n - 1)
        def _():
            halo(c, 1).wait_recv()
            place(high, c, 2 * rows)

    chunk = epochs * 3 * rows

    def stack(k, v):
        sums = [None] * cells
        for e in range(epochs):
            start = LANES + col_ref[e, v]
            skip = start // LANES
            shift = start - skip * LANES
            turn = lax.rem(LANES - shift, LANES)
            base = skip * chunk + e * 3 * rows + rows + row_ref[e, v]
            keep = lane[:rows] < LANES - shift
            turned = [
                pltpu.roll(
                    field[pl.ds(base + (k * (cells + 2) + c) * chunk, rows), :], turn, 1
                )
                for c in range(cells + 1)
            ]
            for c in range(cells):
                piece = jnp.where(keep, turned[c], turned[c + 1])
                sums[c] = piece if e == 0 else sums[c] + piece
        return sums

    def psi_at(v, c):
        return pl.ds(pl.multiple_of((v * cells + c) * rows, rows), rows)

    def psi_stack(v, carry):
        for c, total in enumerate(stack(0, v)):
            psi_sums[psi_at(v, c), :] = total
        return carry

    def phi_stack(v, best):
        sums = stack(1, v)
        return tuple(
            jnp.maximum(
                best[c], psi_sums[psi_at(v, c), :] / jnp.sqrt(jnp.maximum(sums[c], 1.0))
            )
            for c in range(cells)
        )

    for c in range(chunks):
        all_data(c).wait_recv()
        sum_chunk(c)
        start_halo(c)
    finish_halo(0)
    lax.fori_loop(0, vels, psi_stack, 0, unroll=UNROLL)
    for c in range(1, chunks):
        finish_halo(c)

    best = lax.fori_loop(
        0,
        vels,
        phi_stack,
        (jnp.full((rows, LANES), -jnp.inf, jnp.float32),) * cells,
        unroll=UNROLL,
    )
    for c in range(cells):
        out_ref[:, pl.ds(c * LANES, LANES)] = best[c]

    all_codes().wait_send()
    for c in range(chunks):
        all_data(c).wait_send()

    @pl.when(me < n - 1)
    def _():
        for c in range(chunks):
            halo(c, 0).wait_send()

    @pl.when(me > 0)
    def _():
        for c in range(chunks):
            halo(c, 1).wait_send()


def body(psi, phi, dest_tile, dest_cell, kernel_id, weight, kernels, row_offsets, col_offsets):
    n = lax.axis_size("tile")
    cells, epochs, rows, width = psi.shape
    items = cells * epochs
    cap = max(2, 2 * items // n)
    slots = n * cap
    vels = row_offsets.shape[1]
    code_lanes = -(-slots // LANES) * LANES
    pitch = 2 * rows
    f32 = jnp.float32
    return pl.pallas_call(
        functools.partial(
            kernel, (n, cap, cells, epochs, rows, kernels.shape[0], vels)
        ),
        out_shape=pltpu.VMEM((rows, cells * width), f32),
        in_specs=[pl.BlockSpec(memory_space=pl.ANY)] * 9,
        out_specs=pl.BlockSpec(memory_space=pltpu.VMEM),
        scratch_shapes=[
            pltpu.VMEM(psi.shape, f32),
            pltpu.VMEM(phi.shape, f32),
            pltpu.SMEM((cells, epochs), jnp.int32),
            pltpu.SMEM((cells, epochs), jnp.int32),
            pltpu.SMEM((cells, epochs), jnp.int32),
            pltpu.SMEM((cells, epochs), f32),
            pltpu.VMEM(kernels.shape, f32),
            pltpu.SMEM(row_offsets.shape, jnp.int32),
            pltpu.SMEM(col_offsets.shape, jnp.int32),
            pltpu.VMEM((vels * cells * rows, width), f32),
            pltpu.VMEM((3 * kernels.shape[0], width), f32),
            pltpu.VMEM((items * pitch, width), f32),
            pltpu.VMEM((slots * pitch, width), f32),
            pltpu.VMEM((slots * pitch, width), f32),
            pltpu.VMEM((n, 1, code_lanes), f32),
            pltpu.VMEM((n, 1, code_lanes), f32),
            pltpu.VMEM((items * pitch, width), f32),
            pltpu.VMEM((items * pitch, width), f32),
            pltpu.VMEM((items * pitch, width), f32),
            pltpu.VMEM((2 * (cells + 2) * epochs * 3 * rows, width), f32),
            pltpu.SemaphoreType.DMA((9,)),
            pltpu.SemaphoreType.DMA((3,)),
            pltpu.SemaphoreType.DMA((3,)),
            pltpu.SemaphoreType.DMA,
            pltpu.SemaphoreType.DMA,
            pltpu.SemaphoreType.DMA((2, 3)),
            pltpu.SemaphoreType.DMA((2, 3)),
            pltpu.SemaphoreType.REGULAR,
        ],
        compiler_params=pltpu.CompilerParams(collective_id=0, has_side_effects=True),
    )(
        psi,
        phi,
        dest_tile.reshape(cells, epochs),
        dest_cell,
        kernel_id,
        weight,
        kernels,
        row_offsets,
        col_offsets,
    )


def solution(mesh):
    placed = (
        P(("field", "tile"), None, None, None),
        P(("field", "tile"), None, None, None),
        P(("field", "tile"), None, None),
        P(("field", "tile"), None),
        P(("field", "tile"), None),
        P(("field", "tile"), None),
        P(),
        P("field", None),
        P("field", None),
    )
    return jax.shard_map(
        body, mesh=mesh, in_specs=placed, out_specs=P(("field", "tile"), None), check_vma=False
    )
```

time: 26.3 us -> 23.9 us (0.909)
  Pallas kernels: 25.5 us -> 23.1 us
    pallas_call x1, Pallas kernels: 25.5 us -> 23.1 us  [body(): pl.pallas_call(functools.partial(kernel, (n, cap, cells, epochs, rows, ke...]
where the time goes in v1:
time: 23.9 us; the launch traced here: 23.7 us
  Pallas kernels  23.1 us (97%)
  local copies, waits for them, and re-layouts  0.61 us (3%)
    pallas_call x1, Pallas kernels, body(): pl.pallas_call(functools.partial(kernel, (n, cap, cells, epochs, rows, ke...  23.1 us
    unnamed x1, local copies, waits for them, and re-layouts  0.61 us

profile of v1, /device:TPU:1, one launch (start us, length us, event | category | flops | bytes accessed | tf_op | source)
XLA Modules:
  0.0 23.7 jit_solution(1849957086490646582)
XLA Ops:
  0.0 23.1 %shard_map.91 = f32[8,512]{1,0:T(8,128)S(1)} custom-call(f32[4,8,8,128]{3,2,1,0:T(8,128)} %psi_hbm.1, f32[4,8,8,128]{3,2,1,0:T(8,128)} %phi_hbm.1, s32[4,8]{1,0:T(4,128)} %bitcast.1, s32[4,8]{1,0:T(4,128)} %cell_hbm.1, s32[4,8]{1,0:T(4,128)} %kid_hbm.1, f32[4,8]{1,0:T(4,128)} %weight_hbm.1, f32[8,128,128]{2,1,0:T(8,128)} %kern_hbm.1, s32[8,16]{1,0:T(8,128)} %row_hbm.1, ...), custom_call_target="tpu_custom_call" | custom-call | tf_op jit(solution)/shard_map/pallas_call | solution.py:426
  23.1 0.6 %copy.11 = f32[8,512]{1,0:T(8,128)} copy(f32[8,512]{1,0:T(8,128)S(1)} %shard_map.91) | data formatting | bytes 32768

commit v2 on v1

--- a/solution.py
+++ b/solution.py
@@ -63,6 +63,7 @@
     halo_send_sem,
     halo_recv_sem,
     near_sem,
+    shifts,
 ):
     n, cap, cells, epochs, rows, kernels, vels = dims
     items = cells * epochs
@@ -267,6 +268,19 @@
         around(start_data(c))
     for load in loads[7:]:
         load.wait()
+    chunk = epochs * 3 * rows
+
+    def plan(v, carry):
+        for e in range(epochs):
+            start = LANES + col_ref[e, v]
+            shift = start & (LANES - 1)
+            skip = lax.shift_right_logical(start, LANES.bit_length() - 1)
+            shifts[v, e] = skip * chunk + e * 3 * rows + rows + row_ref[e, v]
+            shifts[v, epochs + e] = (LANES - shift) & (LANES - 1)
+            shifts[v, 2 * epochs + e] = LANES - shift
+        return carry
+
+    lax.fori_loop(0, vels, plan, 0)
 
     all_codes().wait_recv()
     code_row = codes_in[0]
@@ -340,17 +354,12 @@
             halo(c, 1).wait_recv()
             place(high, c, 2 * rows)
 
-    chunk = epochs * 3 * rows
-
     def stack(k, v):
         sums = [None] * cells
         for e in range(epochs):
-            start = LANES + col_ref[e, v]
-            skip = start // LANES
-            shift = start - skip * LANES
-            turn = lax.rem(LANES - shift, LANES)
-            base = skip * chunk + e * 3 * rows + rows + row_ref[e, v]
-            keep = lane[:rows] < LANES - shift
+            base = shifts[v, e]
+            turn = shifts[v, epochs + e]
+            keep = lane[:rows] < shifts[v, 2 * epochs + e]
             turned = [
                 pltpu.roll(
                     field[pl.ds(base + (k * (cells + 2) + c) * chunk, rows), :], turn, 1
@@ -459,6 +468,7 @@
             pltpu.SemaphoreType.DMA((2, 3)),
             pltpu.SemaphoreType.DMA((2, 3)),
             pltpu.SemaphoreType.REGULAR,
+            pltpu.SMEM((vels, 3 * epochs), jnp.int32),
         ],
         compiler_params=pltpu.CompilerParams(collective_id=0, has_side_effects=True),
     )(

time: 23.9 us -> 23.4 us (0.979)
  Pallas kernels: 23.1 us -> 22.6 us
    pallas_call x1, Pallas kernels: 23.1 us -> 22.6 us  [body(): pl.pallas_call(functools.partial(kernel, (n, cap, cells, epochs, rows, ke...]
where the time goes in v2:
time: 23.4 us; the launch traced here: 23.2 us
  Pallas kernels  22.6 us (97%)
  local copies, waits for them, and re-layouts  0.61 us (3%)
    pallas_call x1, Pallas kernels, body(): pl.pallas_call(functools.partial(kernel, (n, cap, cells, epochs, rows, ke...  22.6 us
    unnamed x1, local copies, waits for them, and re-layouts  0.61 us

profile of v2, /device:TPU:1, one launch (start us, length us, event | category | flops | bytes accessed | tf_op | source)
XLA Modules:
  0.0 23.2 jit_solution(11907737347579825690)
XLA Ops:
  0.0 22.6 %shard_map.91 = f32[8,512]{1,0:T(8,128)S(1)} custom-call(f32[4,8,8,128]{3,2,1,0:T(8,128)} %psi_hbm.1, f32[4,8,8,128]{3,2,1,0:T(8,128)} %phi_hbm.1, s32[4,8]{1,0:T(4,128)} %bitcast.1, s32[4,8]{1,0:T(4,128)} %cell_hbm.1, s32[4,8]{1,0:T(4,128)} %kid_hbm.1, f32[4,8]{1,0:T(4,128)} %weight_hbm.1, f32[8,128,128]{2,1,0:T(8,128)} %kern_hbm.1, s32[8,16]{1,0:T(8,128)} %row_hbm.1, ...), custom_call_target="tpu_custom_call" | custom-call | tf_op jit(solution)/shard_map/pallas_call | solution.py:435
  22.6 0.6 %copy.11 = f32[8,512]{1,0:T(8,128)} copy(f32[8,512]{1,0:T(8,128)S(1)} %shard_map.91) | data formatting | bytes 32768

commit v3 on v2

--- a/solution.py
+++ b/solution.py
@@ -9,7 +9,7 @@
 
 MESH = pl.DeviceIdType.MESH
 LANES = 128
-UNROLL = 4
+UNROLL = 8
 
 
 def split2(x):
@@ -44,7 +44,7 @@
     kern_ref,
     row_ref,
     col_ref,
-    psi_sums,
+    scales,
     taps,
     moved,
     send,
@@ -106,8 +106,8 @@
         )
     )
 
-    sources = (tile_hbm, cell_hbm, kid_hbm, weight_hbm, kern_hbm, psi_hbm, phi_hbm, row_hbm, col_hbm)
-    places = (tile_ref, cell_ref, kid_ref, weight_ref, kern_ref, psi_ref, phi_ref, row_ref, col_ref)
+    sources = (tile_hbm, cell_hbm, kid_hbm, weight_hbm, kern_hbm, phi_hbm, psi_hbm, row_hbm, col_hbm)
+    places = (tile_ref, cell_ref, kid_ref, weight_ref, kern_ref, phi_ref, psi_ref, row_ref, col_ref)
     loads = [
         pltpu.make_async_copy(source, place, in_sem.at[i])
         for i, (source, place) in enumerate(zip(sources, places))
@@ -194,7 +194,7 @@
         recv[block(c, me), :] = send[block(c, me), :]
 
     loads[5].wait()
-    move(0, psi_ref)
+    move(0, phi_ref)
     pack(0)
     named = jnp.where(
         lax.broadcasted_iota(jnp.int32, (n, LANES), 0) == row_tile[0:1, :],
@@ -262,7 +262,7 @@
     around(start_codes)
     around(start_data(0))
     loads[6].wait()
-    move(1, phi_ref)
+    move(1, psi_ref)
     for c in range(1, chunks):
         pack(c)
         around(start_data(c))
@@ -371,21 +371,18 @@
                 sums[c] = piece if e == 0 else sums[c] + piece
         return sums
 
-    def psi_at(v, c):
+    def scale_at(v, c):
         return pl.ds(pl.multiple_of((v * cells + c) * rows, rows), rows)
 
-    def psi_stack(v, carry):
+    def phi_stack(v, carry):
         for c, total in enumerate(stack(0, v)):
-            psi_sums[psi_at(v, c), :] = total
+            scales[scale_at(v, c), :] = 1.0 / jnp.sqrt(jnp.maximum(total, 1.0))
         return carry
 
-    def phi_stack(v, best):
+    def psi_stack(v, best):
         sums = stack(1, v)
         return tuple(
-            jnp.maximum(
-                best[c], psi_sums[psi_at(v, c), :] / jnp.sqrt(jnp.maximum(sums[c], 1.0))
-            )
-            for c in range(cells)
+            jnp.maximum(best[c], sums[c] * scales[scale_at(v, c), :]) for c in range(cells)
         )
 
     for c in range(chunks):
@@ -393,14 +390,14 @@
         sum_chunk(c)
         start_halo(c)
     finish_halo(0)
-    lax.fori_loop(0, vels, psi_stack, 0, unroll=UNROLL)
+    lax.fori_loop(0, vels, phi_stack, 0, unroll=UNROLL)
     for c in range(1, chunks):
         finish_halo(c)
 
     best = lax.fori_loop(
         0,
         vels,
-        phi_stack,
+        psi_stack,
         (jnp.full((rows, LANES), -jnp.inf, jnp.float32),) * cells,
         unroll=UNROLL,
     )

time: 23.4 us -> 23.2 us (level)
  no operation moved by 1% of the time
where the time goes in v3:
time: 23.2 us; the launch traced here: 23 us
  Pallas kernels  22.4 us (97%)
  local copies, waits for them, and re-layouts  0.61 us (3%)
    pallas_call x1, Pallas kernels, body(): pl.pallas_call(functools.partial(kernel, (n, cap, cells, epochs, rows, ke...  22.4 us
    unnamed x1, local copies, waits for them, and re-layouts  0.61 us

profile of v3, /device:TPU:1, one launch (start us, length us, event | category | flops | bytes accessed | tf_op | source)
XLA Modules:
  0.0 23.0 jit_solution(12227631061838399407)
XLA Ops:
  0.0 22.4 %shard_map.91 = f32[8,512]{1,0:T(8,128)S(1)} custom-call(f32[4,8,8,128]{3,2,1,0:T(8,128)} %psi_hbm.1, f32[4,8,8,128]{3,2,1,0:T(8,128)} %phi_hbm.1, s32[4,8]{1,0:T(4,128)} %bitcast.1, s32[4,8]{1,0:T(4,128)} %cell_hbm.1, s32[4,8]{1,0:T(4,128)} %kid_hbm.1, f32[4,8]{1,0:T(4,128)} %weight_hbm.1, f32[8,128,128]{2,1,0:T(8,128)} %kern_hbm.1, s32[8,16]{1,0:T(8,128)} %row_hbm.1, ...), custom_call_target="tpu_custom_call" | custom-call | tf_op jit(solution)/shard_map/pallas_call | solution.py:432
  22.4 0.6 %copy.11 = f32[8,512]{1,0:T(8,128)} copy(f32[8,512]{1,0:T(8,128)S(1)} %shard_map.91) | data formatting | bytes 32768
